TPU v7x, 512 devices: a whole 4x4x16 slice. The times are simulated.
512 devices in a mesh: layer: 32 (over z, core), dp: 16 (over x, y).
Axes of the slice: x: 4, y: 4, z: 16, core: 2. Of those that a mesh axis runs over, the one named last changes fastest.
Arguments:
- states: bfloat16 [32, 2048, 512], P('layer', 'dp'), may hold values from -6 to 6
- w_in: bfloat16 [64, 512, 1024], P('layer'), may hold values from -0.25 to 0.25
- w_out: bfloat16 [64, 1024, 512], P('layer'), may hold values from -0.1875 to 0.1875
Outputs:
- c_states: bfloat16 [32, 2048, 512], P('layer', 'dp')
- f_states: bfloat16 [32, 2048, 512], P('layer', 'dp')
All inputs are finite; a program needn't handle non-finite values.
Results may differ from a plain program's by a relative error of at most 0.018.
Values may be sent and summed in bfloat16 or wider, within the bound.
A program may use at most 128 MiB of HBM per device.

v0:
```python
import jax
import jax.numpy as jnp
from jax import lax
from jax.sharding import PartitionSpec as P


def passed_along(value, axis, steps):
    count = lax.axis_size(axis)
    initial, last = (max(0, -steps), min(count, count - steps))
    return lax.ppermute(value, axis, [(source, source + steps) for source in range(initial, last)])


def entering(part, axis, combine, identity):
    place = lax.axis_index(axis)
    gathered = jax.tree.map(lambda a: lax.all_gather(a, axis), part)
    state = jax.tree.map(lambda a, e: jnp.zeros_like(a) + jnp.asarray(e, a.dtype), part, identity)

    def one(turn, state):
        return combine(
            state, jax.tree.map(lambda a: lax.dynamic_index_in_dim(a, turn, 0, False), gathered)
        )

    return lax.fori_loop(0, place, one, state)


def advance(state, w_first, w_second):
    inner = jnp.dot(state, w_first, preferred_element_type=jnp.float32)
    gated = jax.nn.gelu(inner, approximate=False).astype(jnp.bfloat16)
    branch = jnp.dot(gated, w_second, preferred_element_type=jnp.float32)
    return (state.astype(jnp.float32) + 0.25 * branch).astype(jnp.bfloat16)


def highest_dot(left, right):
    return jnp.dot(left, right, precision=lax.Precision.HIGHEST, preferred_element_type=jnp.float32)


def compose(earlier, later):
    return (highest_dot(earlier[0], later[0]), highest_dot(earlier[1], later[0]) + later[1])


def shards(states, w_in, w_out):
    given_state = states[0]
    first_in, first_out = (w_in[0], w_out[0])
    second_in, second_out = (w_in[1], w_out[1])
    following = passed_along(given_state, "layer", -1)
    relaxed = advance(given_state, first_in, first_out)
    pushed = advance(relaxed, second_in, second_out)
    defect = pushed.astype(jnp.float32) - following.astype(jnp.float32)
    width = first_in.shape[0]
    row_count = width // lax.axis_size("dp")
    row_block = lax.dynamic_slice_in_dim(first_in, lax.axis_index("dp") * row_count, row_count, 0)
    block_product = jnp.dot(row_block, first_out, preferred_element_type=jnp.float32)
    product = lax.all_gather(block_product, "dp", axis=0, tiled=True)
    identity = jnp.eye(width, dtype=jnp.float32)
    coarse_map = identity + 0.25 * product
    neutral = (identity, jnp.zeros_like(defect))
    _, correction = entering((coarse_map, defect), "layer", compose, neutral)
    corrected = (given_state.astype(jnp.float32) + correction).astype(jnp.bfloat16)
    fine_state = advance(corrected, first_in, first_out)
    return (corrected[None], fine_state[None])


def solution(mesh):
    return jax.shard_map(
        shards,
        mesh=mesh,
        in_specs=(P("layer", "dp", None), P("layer", None, None), P("layer", None, None)),
        out_specs=(P("layer", "dp", None), P("layer", "dp", None)),
        check_vma=False,
    )
```

profile of v0, /device:TPU:481, one launch (start us, length us, event | category | flops | bytes accessed | tf_op | source)
XLA Modules:
  0.0 477.5 jit_solution(14884382239978660157)
XLA Ops:
  13.4 3.1 fusion.7
  16.5 3.5 convert_subtract_fusion
  20.1 46.6 %all-gather.6.cloned.1.call-done = f32[512,512]{1,0:T(8,128)} async-done(((f32[32,512]{1,0:T(8,128)}), f32[512,512]{1,0:T(8,128)}) %all-gather.6.cloned.1.call-update) | async-done | bytes 1048592 | tf_op jit(solution)/shard_map/all_gather | solution.py:53
  69.0 78.9 %all-gather.10.cloned.1.call-done = f32[4096,512]{1,0:T(8,128)} async-done(((f32[128,512]{1,0:T(8,128)}), f32[4096,512]{1,0:T(8,128)}) %all-gather.10.cloned.1.call-update) | async-done | bytes 8388624 | tf_op jit(solution)/shard_map/all_gather | solution.py:15
  147.9 188.5 %all-gather.8.cloned.1.call-done = f32[16384,512]{1,0:T(8,128)} async-done(((f32[512,512]{1,0:T(8,128)}), f32[16384,512]{1,0:T(8,128)}) %all-gather.8.cloned.1.call-update) | async-done | bytes 33554448 | tf_op jit(solution)/shard_map/all_gather | solution.py:15
  336.4 130.2 %while.12 = (s32[]{:T(128)}, f32[128,512]{0,1:T(8,128)S(1)}, s32[]{:T(128)}, f32[32,512,512]{2,1,0:T(8,128)}, f32[32,128,512]{2,1,0:T(8,128)}, /*index=5*/s32[]{:T(128)}, s32[]{:T(128)}, s32[]{:T(128)}) while((s32[]{:T(128)}, f32[128,512]{0,1:T(8,128)S(1)}, s32[]{:T(128)}, f32[32,512,512]{2,1,0:T(8,128)}, f32[32,128,512]{2,1,0:T(8,128)}, ...), condition=%wide.region_1.2_spmd, body=%wide.region_0.1_spmd.sunk | while | flops 402718720 | bytes 3407999 | solution.py:23
  337.6 3.0 fusion.274
  346.0 3.0 fusion.274
  350.2 3.0 fusion.274
  354.4 3.0 fusion.274
  358.6 3.0 fusion.274
  362.8 3.0 fusion.274
  367.0 3.0 fusion.274
  371.2 3.0 fusion.274
  375.4 3.0 fusion.274
  383.8 3.0 fusion.274
  388.0 3.0 fusion.274
  392.2 3.0 fusion.274
  400.6 3.0 fusion.274
  404.8 3.0 fusion.274
  409.0 3.0 fusion.274
  417.4 3.0 fusion.274
  421.6 3.0 fusion.274
  425.8 3.0 fusion.274
  430.0 3.0 fusion.274
  438.4 3.0 fusion.274
  442.6 3.0 fusion.274
  446.8 3.0 fusion.274
  455.2 3.0 fusion.274
  459.4 3.0 fusion.274
  463.6 3.0 fusion.274
  466.8 3.4 fusion.11
  (118 shorter events, 62.1 us)
Async XLA Ops:
  7.2 1.2 slice-start
  7.2 3.4 copy-start.1
  7.2 59.5 %all-gather.6.cloned.1.call-start = ((), (), s32[]{:S(2)}) async-start(), calls=%async_computation | async-start | bytes 1114112 | tf_op jit(solution)/shard_map/all_gather | solution.py:53
  10.6 137.3 %all-gather.10.cloned.1.call-start = ((), (), s32[]{:S(2)}) async-start(), calls=%async_computation.2 | async-start | bytes 8650752 | tf_op jit(solution)/shard_map/all_gather | solution.py:15
  10.6 5.9 %copy-start = (bf16[2,512,1024]{2,1,0:T(8,128)(2,1)S(1)}, bf16[2,512,1024]{2,1,0:T(8,128)(2,1)}, u32[]{:S(2)}) copy-start(bf16[2,512,1024]{2,1,0:T(8,128)(2,1)} %param.6) | copy-start | bytes 6291460
  10.6 5.8 %collective-permute-start = (bf16[128,512]{1,0:T(8,128)(2,1)S(1)}, bf16[128,512]{1,0:T(8,128)(2,1)S(1)}, u32[]{:S(2)}, u32[]{:S(2)}) collective-permute-start(bf16[128,512]{1,0:T(8,128)(2,1)S(1)} %bitcast.76), channel_id=1, source_target_pairs={{16,0},{32,16},{48,32},{64,48},{80,64},{96,80},{112,96},{128,112},... | collective-permute-start | bytes 393224 | tf_op jit(solution)/shard_map/ppermute | solution.py:10
  20.0 316.4 %all-gather.8.cloned.1.call-start = ((), (), s32[]{:S(2)}) async-start(), calls=%async_computation.1 | async-start | bytes 34603008 | tf_op jit(solution)/shard_map/all_gather | solution.py:15
Sparse Core Ops, SparseCore 0:
  11.6 55.0 all-gather.5
  68.8 79.0 all-gather.9
  150.0 186.3 all-gather.7
where the time goes:
time: 480 us; the launch traced here: 477 us
  waiting for transfers between devices  314 us (65%)
  matrix products  106 us (22%)
  local copies, waits for them, and re-layouts  35.9 us (7%)
  between operations  13.8 us (3%)
    all_gather x2, waiting for transfers between devices, entering(): gathered = jax.tree.map(lambda a: lax.all_gather(a, axis), part)  267 us
    dot_general x31, matrix products, highest_dot(): jnp.dot(left, right, precision=lax.Precision.HIGHEST, preferred_element_t...  94.2 us
    all_gather x1, waiting for transfers between devices, shards(): product = lax.all_gather(block_product, 'dp', axis=0, tiled=True)  46.6 us
    dynamic_slice x62, local copies, waits for them, and re-layouts, one(): lax.dynamic_index_in_dim(a, turn, 0, False)  33.9 us
    dot_general x3, matrix products, advance(): branch = jnp.dot(gated, w_second, preferred_element_type=jnp.float32)  10 us
  transfers between devices with their start and end apart: 4, of which 3 were waited for; matrix products, arithmetic and copies ran while one was open for 2% of the time, Pallas kernels for 0%

commit v1 on v0

v1 whole, which is shorter than its diff:
```python
import functools

import jax
import jax.numpy as jnp
from jax import lax
from jax.experimental import pallas as pl
from jax.experimental.pallas import tpu as pltpu
from jax.sharding import PartitionSpec as P

F32, BF16 = jnp.float32, jnp.bfloat16
ROOT_HALF = 0.7071067811865476
CHUNKS = 2


def dot(left, right):
    return jnp.dot(left, right, preferred_element_type=F32)


def gelu(x):
    return 0.5 * x * (1.0 + lax.erf(x * ROOT_HALF))


def advance(state, w_first, w_second):
    gated = gelu(dot(state, w_first)).astype(BF16)
    return (state.astype(F32) + 0.25 * dot(gated, w_second)).astype(BF16)


def kernel(
    layers, states_ref, win_hbm, wout_hbm, c_ref, f_ref,
    win, wout, follow, maps, pair, defect, half_out, half_in, d_all, b_half, carried, leaving,
    load_sem, follow_sems, map_sems, half_sems, chain_send, chain_recv, share_send, share_recv,
):
    me = lax.axis_index("layer")
    core = lax.rem(me, 2)
    partner = me + 1 - 2 * core
    first, last = me < 2, me >= layers - 2
    rows = states_ref.shape[0]
    half = rows // 2
    step = half // CHUNKS
    mine = core * half

    loads = []
    for at in range(2):
        for source, target, slot in ((win_hbm, win, 2 * at), (wout_hbm, wout, 2 * at + 1)):
            load = pltpu.make_async_copy(source.at[at], target.at[at], load_sem.at[slot])
            load.start()
            loads.append(load)

    barrier = pltpu.get_barrier_semaphore()

    def greet(device):
        pl.semaphore_signal(barrier, inc=1, device_id={"layer": device})

    greet(partner)
    beside = me - 1 + 2 * core
    has_beside = jnp.logical_and(beside >= 0, beside < layers)

    @pl.when(has_beside)
    def _():
        greet(beside)

    @pl.when(jnp.logical_not(first))
    def _():
        greet(me - 2)

    @pl.when(jnp.logical_not(last))
    def _():
        greet(me + 2)

    expected = 1 + has_beside.astype(jnp.int32) + (me >= 2).astype(jnp.int32) + (me < layers - 2).astype(jnp.int32)
    pl.semaphore_wait(barrier, expected)

    def remote(source, target, send, recv, device):
        return pltpu.make_async_remote_copy(
            src_ref=source, dst_ref=target, send_sem=send, recv_sem=recv, device_id={"layer": device}
        )

    to_before = remote(states_ref, follow, follow_sems.at[0], follow_sems.at[1], me - 1)

    @pl.when(me > 0)
    def _():
        to_before.start()

    loads[0].wait()
    loads[1].wait()
    width = win.shape[1]
    own_map = maps.at[core]
    own_map[...] = (0.25 * dot(win[0], wout[0])).astype(BF16)
    share_map = remote(own_map, own_map, map_sems.at[0], map_sems.at[1], partner)
    share_map.start()

    state = states_ref[...]
    relaxed = advance(state, win[0], wout[0])
    loads[2].wait()
    loads[3].wait()
    pushed = advance(relaxed, win[1], wout[1])

    @pl.when(me < layers - 1)
    def _():
        to_before.wait_recv()

    @pl.when(me == layers - 1)
    def _():
        follow[...] = jnp.zeros_like(follow)

    defect[...] = pushed.astype(F32) - follow[...].astype(F32)
    half_out[...] = defect[...].astype(BF16)
    share_half = remote(half_out, half_in, half_sems.at[0], half_sems.at[1], partner)
    share_half.start()

    share_map.wait_recv()
    even_map, odd_map = maps[0], maps[1]
    pair[...] = (even_map.astype(F32) + odd_map.astype(F32) + dot(even_map, odd_map)).astype(BF16)
    share_half.wait_recv()

    own_rows = pl.ds(pl.multiple_of(mine, half), half)

    @pl.when(core == 0)
    def _():
        d_all[...] = defect[...]
        b_half[...] = half_in[own_rows, :].astype(F32)

    @pl.when(core == 1)
    def _():
        d_all[...] = half_in[...].astype(F32)
        b_half[...] = defect[own_rows, :]

    even_half = d_all[own_rows, :]
    b_half[...] += even_half + dot(even_half.astype(BF16), maps[1])

    @pl.when(first)
    def _():
        carried[...] = jnp.zeros_like(carried)

    def chunk(at):
        return pl.ds(pl.multiple_of(mine + at * step, step), step)

    hops, shares = [], []
    for at in range(CHUNKS):
        piece = leaving.at[pl.ds(at * step, step), :]
        hops.append(remote(piece, carried.at[chunk(at), :], chain_send.at[at], chain_recv.at[at], me + 2))
        block = carried.at[chunk(at), :]
        shares.append(remote(block, block, share_send.at[at], share_recv.at[at], partner))

    for at in range(CHUNKS):
        @pl.when(jnp.logical_not(first))
        def _(at=at):
            hops[at].wait_recv()
            shares[at].start()

        @pl.when(jnp.logical_not(last))
        def _(at=at):
            here = carried[chunk(at), :]
            ahead = here.astype(F32) + dot(here, pair[...]) + b_half[pl.ds(at * step, step), :]
            leaving[pl.ds(at * step, step), :] = ahead.astype(BF16)
            hops[at].start()

    @pl.when(jnp.logical_not(first))
    def _():
        for share in shares:
            share.wait_recv()

    @pl.when(core == 0)
    def _():
        c_ref[...] = (states_ref[...].astype(F32) + carried[...].astype(F32)).astype(BF16)

    @pl.when(core == 1)
    def _():
        here = carried[...]
        correction = here.astype(F32) + dot(here, maps[0]) + d_all[...]
        c_ref[...] = (states_ref[...].astype(F32) + correction).astype(BF16)

    f_ref[...] = advance(c_ref[...], win[0], wout[0])

    @pl.when(me > 0)
    def _():
        to_before.wait_send()

    share_map.wait_send()
    share_half.wait_send()

    @pl.when(jnp.logical_not(first))
    def _():
        for share in shares:
            share.wait_send()

    @pl.when(jnp.logical_not(last))
    def _():
        for hop in hops:
            hop.wait_send()


def shards(layers, states, w_in, w_out):
    rows, width = states.shape[1:]
    hidden = w_in.shape[2]
    half = rows // 2
    block = jax.ShapeDtypeStruct((rows, width), BF16)
    vmem = pl.BlockSpec(memory_space=pltpu.VMEM)
    hbm = pl.BlockSpec(memory_space=pl.ANY)
    dma = pltpu.SemaphoreType.DMA
    corrected, fine = pl.pallas_call(
        functools.partial(kernel, layers),
        out_shape=(block, block),
        in_specs=[vmem, hbm, hbm],
        out_specs=(vmem, vmem),
        scratch_shapes=[
            pltpu.VMEM((2, width, hidden), BF16),
            pltpu.VMEM((2, hidden, width), BF16),
            pltpu.VMEM((rows, width), BF16),
            pltpu.VMEM((2, width, width), BF16),
            pltpu.VMEM((width, width), BF16),
            pltpu.VMEM((rows, width), F32),
            pltpu.VMEM((rows, width), BF16),
            pltpu.VMEM((rows, width), BF16),
            pltpu.VMEM((rows, width), F32),
            pltpu.VMEM((half, width), F32),
            pltpu.VMEM((rows, width), BF16),
            pltpu.VMEM((half, width), BF16),
            dma((4,)),
            dma((2,)),
            dma((2,)),
            dma((2,)),
            dma((CHUNKS,)),
            dma((CHUNKS,)),
            dma((CHUNKS,)),
            dma((CHUNKS,)),
        ],
        compiler_params=pltpu.CompilerParams(
            collective_id=0, has_side_effects=True, vmem_limit_bytes=48 * 1024 * 1024
        ),
    )(states[0], w_in, w_out)
    return (corrected[None], fine[None])


def solution(mesh):
    return jax.shard_map(
        functools.partial(shards, mesh.shape["layer"]),
        mesh=mesh,
        in_specs=(P("layer", "dp", None), P("layer", None, None), P("layer", None, None)),
        out_specs=(P("layer", "dp", None), P("layer", "dp", None)),
        check_vma=False,
    )
```

time: 480 us -> 61.6 us (0.13)
  waiting for transfers between devices: 314 us -> 0 us
  matrix products: 106 us -> 0 us
  Pallas kernels: 0 us -> 55.4 us
  local copies, waits for them, and re-layouts: 35.9 us -> 5.39 us
  between operations: 13.8 us -> 0.65 us
    all_gather x3 -> x0, waiting for transfers between devices: 314 us -> none  [the longest x2 267 us: entering(): gathered = jax.tree.map(lambda a: lax.all_gather(a, axis), part)]
    dot_general x35 -> x0, matrix products: 106 us -> none  [the longest x31 94.2 us: highest_dot(): jnp.dot(left, right, precision=lax.Precision.HIGHEST, preferred_element_t...]
    pallas_call x0 -> x1, Pallas kernels: none -> 55.4 us  [shards(): pl.pallas_call(functools.partial(kernel, layers), out_shape=(block, block...]
    dynamic_slice x62 -> x0, local copies, waits for them, and re-layouts: 33.9 us -> none  [one(): lax.dynamic_index_in_dim(a, turn, 0, False)]
    unnamed x4 -> x8, local copies, waits for them, and re-layouts: 0.01 us -> 5.39 us
  transfers between devices with their start and end apart: 4 -> 0, of which waited for: 3 -> 0; matrix products, arithmetic and copies ran while one was open for 2% -> 0% of each run, Pallas kernels for 0% -> 0%
where the time goes in v1:
time: 61.6 us; the launch traced here: 61.4 us
  Pallas kernels  55.4 us (90%)
  local copies, waits for them, and re-layouts  5.39 us (9%)
  between operations  0.65 us (1%)
    pallas_call x1, Pallas kernels, shards(): pl.pallas_call(functools.partial(kernel, layers), out_shape=(block, block...  55.4 us
    unnamed x8, local copies, waits for them, and re-layouts  5.39 us

profile of v1, /device:TPU:481, one launch (start us, length us, event | category | flops | bytes accessed | tf_op | source)
XLA Modules:
  0.0 61.4 jit_solution(2071927586827788354)
XLA Ops:
  0.6 0.0 copy-start
  0.6 1.6 %copy-done = bf16[2,512,1024]{2,1,0:T(8,128)(2,1)S(1)} copy-done((bf16[2,512,1024]{2,1,0:T(8,128)(2,1)S(1)}, bf16[2,512,1024]{2,1,0:T(8,128)(2,1)}, u32[]{:S(2)}) %copy-start) | copy-done | bytes 2097176
  2.2 0.0 copy-start.1
  2.2 1.6 %copy-done.1 = bf16[2,1024,512]{2,1,0:T(8,128)(2,1)S(1)} copy-done((bf16[2,1024,512]{2,1,0:T(8,128)(2,1)S(1)}, bf16[2,1024,512]{2,1,0:T(8,128)(2,1)}, u32[]{:S(2)}) %copy-start.1) | copy-done | bytes 2097176
  3.8 0.0 copy-start.2
  3.8 0.9 %copy-done.2 = bf16[1,128,512]{2,1,0:T(8,128)(2,1)S(1)} copy-done((bf16[1,128,512]{2,1,0:T(8,128)(2,1)S(1)}, bf16[1,128,512]{2,1,0:T(8,128)(2,1)}, u32[]{:S(2)}) %copy-start.2) | copy-done | bytes 131096
  4.7 55.4 %shard_map.50 = (bf16[128,512]{1,0:T(8,128)(2,1)S(1)}, bf16[128,512]{1,0:T(8,128)(2,1)S(1)}) custom-call(bf16[128,512]{1,0:T(8,128)(2,1)S(1)} %bitcast.3, bf16[2,512,1024]{2,1,0:T(8,128)(2,1)S(1)} %copy-done, bf16[2,1024,512]{2,1,0:T(8,128)(2,1)S(1)} %copy-done.1), custom_call_target="tpu_custom_call" | custom-call | tf_op jit(solution)/shard_map/pallas_call | solution.py:201
  60.1 0.7 %copy.7 = bf16[1,128,512]{2,1,0:T(8,128)(2,1)} copy(bf16[1,128,512]{2,1,0:T(8,128)(2,1)S(1)} %bitcast.5) | data formatting | bytes 262144
  60.8 0.7 %copy.8 = bf16[1,128,512]{2,1,0:T(8,128)(2,1)} copy(bf16[1,128,512]{2,1,0:T(8,128)(2,1)S(1)} %bitcast.4) | data formatting | bytes 262144
Async XLA Ops:
  0.6 1.6 %copy-start = (bf16[2,512,1024]{2,1,0:T(8,128)(2,1)S(1)}, bf16[2,512,1024]{2,1,0:T(8,128)(2,1)}, u32[]{:S(2)}) copy-start(bf16[2,512,1024]{2,1,0:T(8,128)(2,1)} %win_hbm.1) | copy-start | bytes 6291460
  2.2 1.6 %copy-start.1 = (bf16[2,1024,512]{2,1,0:T(8,128)(2,1)S(1)}, bf16[2,1024,512]{2,1,0:T(8,128)(2,1)}, u32[]{:S(2)}) copy-start(bf16[2,1024,512]{2,1,0:T(8,128)(2,1)} %wout_hbm.1) | copy-start | bytes 6291460
  3.8 0.9 %copy-start.2 = (bf16[1,128,512]{2,1,0:T(8,128)(2,1)S(1)}, bf16[1,128,512]{2,1,0:T(8,128)(2,1)}, u32[]{:S(2)}) copy-start(bf16[1,128,512]{2,1,0:T(8,128)(2,1)} %param.3) | copy-start | bytes 393220

commit v2 on v1

v2 whole, which is shorter than its diff:
```python
import functools

import jax
import jax.numpy as jnp
from jax import lax
from jax.experimental import pallas as pl
from jax.experimental.pallas import tpu as pltpu
from jax.sharding import PartitionSpec as P

F32, BF16 = jnp.float32, jnp.bfloat16
ROOT_HALF = 0.7071067811865476
CHUNKS = 2


def groups_of(chips):
    if chips == 16:
        return (4, 4, 5, 3)
    return tuple([max(1, chips // 3)] * 2 + [chips - 2 * max(1, chips // 3)])


def dot(left, right):
    return jnp.dot(left, right, preferred_element_type=F32)


def gelu(x):
    return 0.5 * x * (1.0 + lax.erf(x * ROOT_HALF))


def advance(state, w_first, w_second):
    gated = gelu(dot(state, w_first)).astype(BF16)
    return (state.astype(F32) + 0.25 * dot(gated, w_second)).astype(BF16)


def kernel(
    layers, columns, states_ref, win_hbm, wout_hbm, c_ref, f_ref,
    win, wout, follow, maps, pair, defect, half_out, half_in, d_all, b_half, carried,
    local_in, local_out, x_in, x_out, prefix, e_in, e_out, c_half,
    load_sem, follow_sems, map_sems, half_sems, x_sems, gather_send, gather_recv, swap_sems,
    local_send, local_recv, e_send, e_recv, share_send, share_recv,
):
    me, column = lax.axis_index("layer"), lax.axis_index("dp")
    core, chip = lax.rem(me, 2), me // 2
    partner = me + 1 - 2 * core
    rows, width = states_ref.shape
    half, half_width = rows // 2, width // 2
    step = half // CHUNKS
    part = half_width // columns
    mine = core * half

    sizes = groups_of(layers // 2)
    widest = max(sizes[1:])
    start, size, following_size, at = 0, sizes[0], sizes[1], 0
    for k in range(1, len(sizes)):
        at += sizes[k - 1]
        reached = (chip >= at).astype(jnp.int32)
        ahead = sizes[k + 1] if k + 1 < len(sizes) else 0
        start = start + reached * sizes[k - 1]
        size = size + reached * (sizes[k] - sizes[k - 1])
        following_size = following_size + reached * (ahead - sizes[k])
    number = lambda flag: flag.astype(jnp.int32)
    opens = chip == start
    closes = chip == start + size - 1
    later = chip >= sizes[0]
    recv_local, send_local = jnp.logical_not(opens), jnp.logical_not(closes)
    recv_x, send_x = jnp.logical_and(recv_local, later), jnp.logical_and(send_local, later)
    send_e = jnp.logical_and(closes, following_size > 0)

    loads = []
    for at in range(2):
        for source, target, slot in ((win_hbm, win, 2 * at), (wout_hbm, wout, 2 * at + 1)):
            load = pltpu.make_async_copy(source.at[at], target.at[at], load_sem.at[slot])
            load.start()
            loads.append(load)

    barrier = pltpu.get_barrier_semaphore()
    send_back = jnp.logical_and(core == 0, me > 0)
    recv_back = jnp.logical_and(core == 1, me < layers - 1)

    def greet(**device):
        pl.semaphore_signal(barrier, inc=1, device_id=device)

    greet(layer=partner)

    @pl.when(recv_back)
    def _():
        greet(layer=me + 1)

    @pl.when(recv_local)
    def _():
        greet(layer=me - 2)

    @pl.when(later)
    def _():
        greet(layer=2 * (start - 1) + core)

    peers = [lax.rem(column + turn, columns) for turn in range(1, columns)]

    @pl.when(recv_x)
    def _():
        for peer in peers:
            greet(dp=peer)

    def remote(source, target, send, recv, **device):
        return pltpu.make_async_remote_copy(
            src_ref=source, dst_ref=target, send_sem=send, recv_sem=recv, device_id=device
        )

    loads[0].wait()
    loads[1].wait()
    own_map = maps.at[core]
    own_map[...] = (0.25 * dot(win[0], wout[0])).astype(BF16)

    pl.semaphore_wait(
        barrier,
        1 + number(send_back) + number(send_local) + number(send_e) * following_size
        + number(recv_x) * (columns - 1),
    )
    share_map = remote(own_map, own_map, map_sems.at[0], map_sems.at[1], layer=partner)
    share_map.start()
    to_before = remote(states_ref, follow, follow_sems.at[0], follow_sems.at[1], layer=me - 1)

    @pl.when(me > 0)
    def _():
        to_before.start()

    state = states_ref[...]
    relaxed = advance(state, win[0], wout[0])

    share_map.wait_recv()
    even_map, odd_map = maps[0], maps[1]
    pair[...] = (even_map.astype(F32) + odd_map.astype(F32) + dot(even_map, odd_map)).astype(BF16)

    own_part = pl.ds(pl.multiple_of(core * half_width + column * part, part), part)
    x_hop = remote(x_out, x_in, x_sems.at[0], x_sems.at[1], layer=me + 2)
    gathers = [
        remote(x_in, prefix.at[own_part, :], gather_send.at[turn], gather_recv, dp=peer)
        for turn, peer in enumerate(peers)
    ]
    half_prefix = prefix.at[pl.ds(pl.multiple_of(core * half_width, half_width), half_width), :]
    swap = remote(half_prefix, half_prefix, swap_sems.at[0], swap_sems.at[1], layer=partner)

    def x_step(received):
        ahead = pair[own_part, :].astype(F32)
        if received:
            x = x_in[...]
            ahead = ahead + x.astype(F32) + dot(x, pair[...])
        x_out[...] = ahead.astype(BF16)
        x_hop.start()

    @pl.when(jnp.logical_and(send_x, opens))
    def _():
        x_step(False)

    loads[2].wait()
    loads[3].wait()
    pushed = advance(relaxed, win[1], wout[1])

    @pl.when(me < layers - 1)
    def _():
        to_before.wait_recv()

    @pl.when(me == layers - 1)
    def _():
        follow[...] = jnp.zeros_like(follow)

    defect[...] = pushed.astype(F32) - follow[...].astype(F32)
    half_out[...] = defect[...].astype(BF16)
    share_half = remote(half_out, half_in, half_sems.at[0], half_sems.at[1], layer=partner)
    share_half.start()
    share_half.wait_recv()

    own_rows = pl.ds(pl.multiple_of(mine, half), half)

    @pl.when(core == 0)
    def _():
        d_all[...] = defect[...]
        b_half[...] = half_in[own_rows, :].astype(F32)

    @pl.when(core == 1)
    def _():
        d_all[...] = half_in[...].astype(F32)
        b_half[...] = defect[own_rows, :]

    even_half = d_all[own_rows, :]
    b_half[...] += even_half + dot(even_half.astype(BF16), maps[1])

    spans = [pl.ds(at * step, step) for at in range(CHUNKS)]
    local_hops = [
        remote(local_out.at[span, :], local_in.at[span, :], local_send.at[at], local_recv.at[at], layer=me + 2)
        for at, span in enumerate(spans)
    ]

    @pl.when(opens)
    def _():
        local_in[...] = jnp.zeros_like(local_in)

        @pl.when(send_local)
        def _():
            local_out[...] = b_half[...].astype(BF16)
            for hop in local_hops:
                hop.start()

    @pl.when(recv_x)
    def _():
        x_hop.wait_recv()

        @pl.when(send_x)
        def _():
            x_step(True)

        for gather in gathers:
            gather.start()
        prefix[own_part, :] = x_in[...]

    @pl.when(recv_local)
    def _():
        for at, span in enumerate(spans):
            local_hops[at].wait_recv()

            @pl.when(send_local)
            def _(at=at, span=span):
                here = local_in[span, :]
                ahead = here.astype(F32) + dot(here, pair[...]) + b_half[span, :]
                local_out[span, :] = ahead.astype(BF16)
                local_hops[at].start()

    @pl.when(recv_x)
    def _():
        landed = prefix.at[pl.ds(0, (columns - 1) * part), :]
        remote(landed, landed, gather_send.at[0], gather_recv, layer=partner).wait_recv()
        swap.start()
        swap.wait_recv()

    def chunk(at):
        return pl.ds(pl.multiple_of(mine + at * step, step), step)

    shares = [
        remote(carried.at[chunk(at), :], carried.at[chunk(at), :], share_send.at[at], share_recv.at[at], layer=partner)
        for at in range(CHUNKS)
    ]
    e_hops = [
        [
            remote(
                e_out.at[span, :], e_in.at[span, :], e_send.at[(away - 1) * CHUNKS + at], e_recv.at[at],
                layer=me + 2 * away,
            )
            for at, span in enumerate(spans)
        ]
        for away in range(1, widest + 1)
    ]

    for at, span in enumerate(spans):
        @pl.when(jnp.logical_not(later))
        def _(at=at, span=span):
            carried[chunk(at), :] = local_in[span, :]
            c_half[span, :] = local_in[span, :].astype(F32)

        @pl.when(later)
        def _(at=at, span=span):
            e_hops[0][at].wait_recv()

            @pl.when(opens)
            def _():
                carried[chunk(at), :] = e_in[span, :]
                c_half[span, :] = e_in[span, :].astype(F32)

            @pl.when(recv_local)
            def _():
                here = e_in[span, :]
                total = local_in[span, :].astype(F32) + here.astype(F32) + dot(here, prefix[...])
                carried[chunk(at), :] = total.astype(BF16)
                c_half[span, :] = total

        shares[at].start()

        @pl.when(send_e)
        def _(at=at, span=span):
            ahead = c_half[span, :] + dot(carried[chunk(at), :], pair[...]) + b_half[span, :]
            e_out[span, :] = ahead.astype(BF16)
            for away in range(1, widest + 1):
                @pl.when(following_size == away)
                def _(away=away):
                    e_hops[away - 1][at].start()

    @pl.when(send_e)
    def _():
        for away in range(widest - 1, 0, -1):
            @pl.when(following_size > away)
            def _(away=away):
                for hop in e_hops[away - 1]:
                    hop.start()

    def finish(offset):
        span = pl.ds(pl.multiple_of(offset, half), half)

        @pl.when(core == 0)
        def _():
            c_ref[span, :] = (states_ref[span, :].astype(F32) + carried[span, :].astype(F32)).astype(BF16)

        @pl.when(core == 1)
        def _():
            here = carried[span, :]
            correction = here.astype(F32) + dot(here, maps[0]) + d_all[span, :]
            c_ref[span, :] = (states_ref[span, :].astype(F32) + correction).astype(BF16)

        f_ref[span, :] = advance(c_ref[span, :], win[0], wout[0])

    finish(mine)
    for share in shares:
        share.wait_recv()
    finish(half - mine)

    share_map.wait_send()
    share_half.wait_send()
    for share in shares:
        share.wait_send()

    @pl.when(me > 0)
    def _():
        to_before.wait_send()

    @pl.when(send_x)
    def _():
        x_hop.wait_send()

    @pl.when(recv_x)
    def _():
        for gather in gathers:
            gather.wait_send()
        swap.wait_send()

    @pl.when(send_local)
    def _():
        for hop in local_hops:
            hop.wait_send()

    @pl.when(send_e)
    def _():
        for away in range(1, widest + 1):
            @pl.when(following_size >= away)
            def _(away=away):
                for hop in e_hops[away - 1]:
                    hop.wait_send()


def shards(layers, columns, states, w_in, w_out):
    rows, width = states.shape[1:]
    hidden = w_in.shape[2]
    half = rows // 2
    part = width // (2 * columns)
    widest = max(groups_of(layers // 2)[1:])
    block = jax.ShapeDtypeStruct((rows, width), BF16)
    vmem = pl.BlockSpec(memory_space=pltpu.VMEM)
    hbm = pl.BlockSpec(memory_space=pl.ANY)
    dma = pltpu.SemaphoreType.DMA
    corrected, fine = pl.pallas_call(
        functools.partial(kernel, layers, columns),
        out_shape=(block, block),
        in_specs=[vmem, hbm, hbm],
        out_specs=(vmem, vmem),
        scratch_shapes=[
            pltpu.VMEM((2, width, hidden), BF16),
            pltpu.VMEM((2, hidden, width), BF16),
            pltpu.VMEM((rows, width), BF16),
            pltpu.VMEM((2, width, width), BF16),
            pltpu.VMEM((width, width), BF16),
            pltpu.VMEM((rows, width), F32),
            pltpu.VMEM((rows, width), BF16),
            pltpu.VMEM((rows, width), BF16),
            pltpu.VMEM((rows, width), F32),
            pltpu.VMEM((half, width), F32),
            pltpu.VMEM((rows, width), BF16),
            pltpu.VMEM((half, width), BF16),
            pltpu.VMEM((half, width), BF16),
            pltpu.VMEM((part, width), BF16),
            pltpu.VMEM((part, width), BF16),
            pltpu.VMEM((width, width), BF16),
            pltpu.VMEM((half, width), BF16),
            pltpu.VMEM((half, width), BF16),
            pltpu.VMEM((half, width), F32),
            dma((4,)),
            dma((2,)),
            dma((2,)),
            dma((2,)),
            dma((2,)),
            dma((columns,)),
            dma,
            dma((2,)),
            dma((CHUNKS,)),
            dma((CHUNKS,)),
            dma((widest * CHUNKS,)),
            dma((CHUNKS,)),
            dma((CHUNKS,)),
            dma((CHUNKS,)),
        ],
        compiler_params=pltpu.CompilerParams(
            collective_id=0, has_side_effects=True, vmem_limit_bytes=67043328
        ),
    )(states[0], w_in, w_out)
    return (corrected[None], fine[None])


def solution(mesh):
    return jax.shard_map(
        functools.partial(shards, mesh.shape["layer"], mesh.shape["dp"]),
        mesh=mesh,
        in_specs=(P("layer", "dp", None), P("layer", None, None), P("layer", None, None)),
        out_specs=(P("layer", "dp", None), P("layer", "dp", None)),
        check_vma=False,
    )
```

time: 61.6 us -> 41.9 us (0.68)
  the two profiles are of different devices: /device:TPU:481 before, /device:TPU:417 now
where the time goes in v2:
time: 41.9 us; the launch traced here: 41.7 us
  Pallas kernels  37.9 us (90%)
  local copies, waits for them, and re-layouts  3.14 us (7%)
  between operations  0.64 us (2%)
    pallas_call x1, Pallas kernels, shards(): pl.pallas_call(functools.partial(kernel, layers, columns), out_shape=(blo...  37.9 us
    unnamed x2, local copies, waits for them, and re-layouts  3.14 us

profile of v2, /device:TPU:417, one launch (start us, length us, event | category | flops | bytes accessed | tf_op | source)
XLA Modules:
  0.0 41.7 jit_solution(1594002196346009213)
XLA Ops:
  0.6 37.9 %shard_map.50 = (bf16[128,512]{1,0:T(8,128)(2,1)}, bf16[128,512]{1,0:T(8,128)(2,1)}) custom-call(bf16[128,512]{1,0:T(8,128)(2,1)} %bitcast.3, bf16[2,512,1024]{2,1,0:T(8,128)(2,1)} %win_hbm.1, bf16[2,1024,512]{2,1,0:T(8,128)(2,1)} %wout_hbm.1), custom_call_target="tpu_custom_call" | custom-call | tf_op jit(solution)/shard_map/pallas_call | solution.py:356
  38.6 1.6 %copy.7 = bf16[1,128,512]{2,1,0:T(8,128)(2,1)} copy(bf16[1,128,512]{2,1,0:T(8,128)(2,1)} %bitcast.5) | data formatting | bytes 262144
  40.1 1.6 %copy.8 = bf16[1,128,512]{2,1,0:T(8,128)(2,1)} copy(bf16[1,128,512]{2,1,0:T(8,128)(2,1)} %bitcast.4) | data formatting | bytes 262144

commit v3 on v2

v3 whole, which is shorter than its diff:
```python
import functools

import jax
import jax.numpy as jnp
from jax import lax
from jax.experimental import pallas as pl
from jax.experimental.pallas import tpu as pltpu
from jax.sharding import PartitionSpec as P

F32, BF16 = jnp.float32, jnp.bfloat16
ROOT_HALF = 0.7071067811865476
CHUNKS = 2


def groups_of(chips):
    if chips == 16:
        return (4, 3, 5, 4)
    return (chips // 3, chips // 3, chips - 2 * (chips // 3))


def dot(left, right):
    return jnp.dot(left, right, preferred_element_type=F32)


def gelu(x):
    return 0.5 * x * (1.0 + lax.erf(x * ROOT_HALF))


def advance(state, w_first, w_second):
    gated = gelu(dot(state, w_first)).astype(BF16)
    return (state.astype(F32) + 0.25 * dot(gated, w_second)).astype(BF16)


def kernel(
    layers, columns, states_hbm, win_hbm, wout_hbm, c_hbm, f_hbm,
    state, win, wout, follow, maps, pair, defect, half_out, half_in, d_all, b_half, carried,
    local_in, local_out, x_in, x_out, prefix, jump, base, e_in, e_out, c_buf, f_buf,
    load_sem, follow_sems, map_sems, half_sems, x_sems, gather_send, gather_recv, swap_sems,
    local_send, local_recv, e_send, e_recv, share_send, share_recv, store_sem, hello, plane,
):
    me, column = lax.axis_index("layer"), lax.axis_index("dp")
    core, chip = lax.rem(me, 2), me // 2
    partner = me + 1 - 2 * core
    rows, width = state.shape
    half, half_width = rows // 2, width // 2
    step = half // CHUNKS
    part = half_width // columns
    mine = core * half
    both, neither = jnp.logical_and, jnp.logical_not

    sizes = groups_of(layers // 2)
    widest = max(sizes[1:])
    start, size, following_size, at = 0, sizes[0], sizes[1], 0
    for k in range(1, len(sizes)):
        at += sizes[k - 1]
        reached = (chip >= at).astype(jnp.int32)
        ahead = sizes[k + 1] if k + 1 < len(sizes) else 0
        start = start + reached * sizes[k - 1]
        size = size + reached * (sizes[k] - sizes[k - 1])
        following_size = following_size + reached * (ahead - sizes[k])
    to_close = start + size - 1 - chip
    opens, closes = chip == start, to_close == 0
    later, first, last = chip >= sizes[0], chip == 0, chip == layers // 2 - 1
    recv_local, send_local = neither(opens), neither(closes)
    recv_x, send_x = both(recv_local, later), both(send_local, later)
    send_e = both(closes, following_size > 0)
    send_map, recv_map = me > 0, me != 1

    def number(flag):
        return flag.astype(jnp.int32)

    def remote(source, target, send, recv, **device):
        return pltpu.make_async_remote_copy(
            src_ref=source, dst_ref=target, send_sem=send, recv_sem=recv, device_id=device
        )

    loads = [
        pltpu.make_async_copy(source, target, load_sem.at[slot])
        for slot, (source, target) in enumerate((
            (win_hbm.at[0], win.at[0]),
            (wout_hbm.at[0], wout.at[0]),
            (states_hbm, state),
            (win_hbm.at[1], win.at[1]),
            (wout_hbm.at[1], wout.at[1]),
        ))
    ]
    for load in loads:
        load.start()

    barrier = pltpu.get_barrier_semaphore()
    send_back = both(core == 0, me > 0)
    recv_back = both(core == 1, me < layers - 1)

    def greet(**device):
        pl.semaphore_signal(barrier, inc=1, device_id=device)

    greet(layer=partner)

    @pl.when(recv_back)
    def _():
        greet(layer=me + 1)

    @pl.when(neither(first))
    def _():
        greet(layer=me - 2)

    @pl.when(neither(last))
    def _():
        greet(layer=me + 2)

    side = 4 if columns % 4 == 0 else 1
    depth = columns // side
    line, place = column // depth, lax.rem(column, depth)
    in_line = [line * depth + lax.rem(place + turn, depth) for turn in range(1, depth)]
    across = [lax.rem(line + turn, side) * depth + place for turn in range(1, side)]

    @pl.when(recv_x)
    def _():
        for peer in in_line + across:
            greet(dp=peer)

    loads[0].wait()
    loads[1].wait()
    own_map = maps.at[core]

    @pl.when(send_map)
    def _():
        own_map[...] = (0.25 * dot(win[0], wout[0])).astype(BF16)

    loads[2].wait()
    pl.semaphore_wait(
        barrier,
        1 + number(send_back) + number(neither(first)) + number(neither(last))
        + number(recv_x) * (len(in_line) + len(across)),
    )
    share_map = remote(own_map, own_map, map_sems.at[0], map_sems.at[1], layer=partner)

    @pl.when(send_map)
    def _():
        share_map.start()

    to_before = remote(state, follow, follow_sems.at[0], follow_sems.at[1], layer=me - 1)

    @pl.when(me > 0)
    def _():
        to_before.start()

    @pl.when(recv_x)
    def _():
        for peer in across:
            pl.semaphore_signal(plane, inc=1, device_id={"dp": peer})

    def pass_hello(turn):
        @pl.when(both(to_close == turn, neither(first)))
        def _():
            if turn > 0:
                pl.semaphore_wait(hello, 1)
            pl.semaphore_signal(hello, inc=1, device_id={"layer": me - 2})

    @pl.when(both(first, neither(closes)))
    def _():
        pl.semaphore_wait(hello, 1)

    pass_hello(0)
    relaxed = advance(state[...], win[0], wout[0])
    pass_hello(1)

    loads[3].wait()
    loads[4].wait()
    pushed = advance(relaxed, win[1], wout[1])

    @pl.when(me < layers - 1)
    def _():
        to_before.wait_recv()

    @pl.when(me == layers - 1)
    def _():
        follow[...] = jnp.zeros_like(follow)

    defect[...] = pushed.astype(F32) - follow[...].astype(F32)
    half_out[...] = defect[...].astype(BF16)
    share_half = remote(half_out, half_in, half_sems.at[0], half_sems.at[1], layer=partner)
    share_half.start()
    pass_hello(2)

    @pl.when(recv_map)
    def _():
        share_map.wait_recv()

    @pl.when(neither(first))
    def _():
        even_map, odd_map = maps[0], maps[1]
        pair[...] = (even_map.astype(F32) + odd_map.astype(F32) + dot(even_map, odd_map)).astype(BF16)

    own_part = pl.ds(pl.multiple_of(core * half_width + column * part, part), part)
    x_hop = remote(x_out, x_in, x_sems.at[0], x_sems.at[1], layer=me + 2)
    peers = [lax.rem(column + turn, columns) for turn in range(1, columns)]
    gathers = [
        remote(x_in, prefix.at[own_part, :], gather_send.at[turn], gather_recv, dp=peer)
        for turn, peer in enumerate(peers)
    ]
    half_prefix = prefix.at[pl.ds(pl.multiple_of(core * half_width, half_width), half_width), :]
    swap = remote(half_prefix, half_prefix, swap_sems.at[0], swap_sems.at[1], layer=partner)

    @pl.when(both(send_x, opens))
    def _():
        x_out[...] = pair[own_part, :]
        x_hop.start()

    pass_hello(3)
    share_half.wait_recv()
    own_rows = pl.ds(pl.multiple_of(mine, half), half)

    @pl.when(core == 0)
    def _():
        d_all[...] = defect[...]
        b_half[...] = half_in[own_rows, :].astype(F32)

    @pl.when(core == 1)
    def _():
        d_all[...] = half_in[...].astype(F32)
        b_half[...] = defect[own_rows, :]

    even_half = d_all[own_rows, :]
    b_half[...] += even_half + dot(even_half.astype(BF16), maps[1])

    spans = [pl.ds(at * step, step) for at in range(CHUNKS)]
    local_hops = [
        remote(local_out.at[span, :], local_in.at[span, :], local_send.at[at], local_recv.at[at], layer=me + 2)
        for at, span in enumerate(spans)
    ]
    e_hops = [
        [
            remote(
                e_out.at[span, :], e_in.at[span, :], e_send.at[(away - 1) * CHUNKS + at], e_recv.at[at],
                layer=me + 2 * away,
            )
            for at, span in enumerate(spans)
        ]
        for away in range(1, widest + 1)
    ]

    def send_far(at):
        for away in range(1, widest + 1):
            @pl.when(following_size == away)
            def _(away=away):
                e_hops[away - 1][at].start()

    def send_others():
        for away in range(widest - 1, 0, -1):
            @pl.when(following_size > away)
            def _(away=away):
                for hop in e_hops[away - 1]:
                    hop.start()

    @pl.when(opens)
    def _():
        local_out[...] = b_half[...].astype(BF16)
        for hop in local_hops:
            hop.start()

    pass_hello(4)

    @pl.when(recv_x)
    def _():
        x_hop.wait_recv()

        @pl.when(send_x)
        def _():
            x = x_in[...]
            x_out[...] = (pair[own_part, :].astype(F32) + x.astype(F32) + dot(x, pair[...])).astype(BF16)
            x_hop.start()

        if across:
            pl.semaphore_wait(plane, len(across))
        for gather in gathers:
            gather.start()
        prefix[own_part, :] = x_in[...]

    @pl.when(send_e)
    def _():
        pl.semaphore_wait(hello, 1)

    @pl.when(recv_local)
    def _():
        for at, span in enumerate(spans):
            local_hops[at].wait_recv()

            @pl.when(neither(last))
            def _(at=at, span=span):
                here = local_in[span, :]
                ahead = here.astype(F32) + dot(here, pair[...]) + b_half[span, :]

                @pl.when(send_local)
                def _():
                    local_out[span, :] = ahead.astype(BF16)
                    local_hops[at].start()

                @pl.when(both(closes, later))
                def _():
                    base[span, :] = ahead

                @pl.when(both(closes, neither(later)))
                def _():
                    e_out[span, :] = ahead.astype(BF16)
                    send_far(at)

    @pl.when(both(closes, neither(later)))
    def _():
        send_others()

    @pl.when(recv_x)
    def _():
        landed = prefix.at[pl.ds(0, (columns - 1) * part), :]
        remote(landed, landed, gather_send.at[0], gather_recv, layer=partner).wait_recv()
        swap.start()
        swap.wait_recv()

        @pl.when(send_e)
        def _():
            whole = prefix[...]
            jump[...] = (whole.astype(F32) + pair[...].astype(F32) + dot(whole, pair[...])).astype(BF16)

    def chunk(at):
        return pl.ds(pl.multiple_of(mine + at * step, step), step)

    shares = [
        remote(carried.at[chunk(at), :], carried.at[chunk(at), :], share_send.at[at], share_recv.at[at], layer=partner)
        for at in range(CHUNKS)
    ]

    @pl.when(first)
    def _():
        carried[...] = jnp.zeros_like(carried)

    @pl.when(both(neither(later), neither(first)))
    def _():
        for at, span in enumerate(spans):
            carried[chunk(at), :] = local_in[span, :]
            shares[at].start()

    def with_entering(at, span):
        here = e_in[span, :]

        @pl.when(opens)
        def _():
            carried[chunk(at), :] = here

        @pl.when(recv_local)
        def _():
            total = local_in[span, :].astype(F32) + here.astype(F32) + dot(here, prefix[...])
            carried[chunk(at), :] = total.astype(BF16)

        shares[at].start()

    @pl.when(both(later, send_e))
    def _():
        for at, span in enumerate(spans):
            e_hops[0][at].wait_recv()
            here = e_in[span, :]
            ahead = base[span, :] + here.astype(F32) + dot(here, jump[...])
            e_out[span, :] = ahead.astype(BF16)
            send_far(at)
        send_others()
        for at, span in enumerate(spans):
            with_entering(at, span)

    @pl.when(both(later, neither(send_e)))
    def _():
        for at, span in enumerate(spans):
            e_hops[0][at].wait_recv()
            with_entering(at, span)

    stores = []

    def finish(offset, slot):
        span = pl.ds(pl.multiple_of(offset, half), half)

        @pl.when(core == 0)
        def _():
            c_buf[span, :] = (state[span, :].astype(F32) + carried[span, :].astype(F32)).astype(BF16)

        @pl.when(both(core == 1, neither(first)))
        def _():
            here = carried[span, :]
            correction = here.astype(F32) + dot(here, maps[0]) + d_all[span, :]
            c_buf[span, :] = (state[span, :].astype(F32) + correction).astype(BF16)

        @pl.when(both(core == 1, first))
        def _():
            c_buf[span, :] = (state[span, :].astype(F32) + d_all[span, :]).astype(BF16)

        for buffer, out, at in ((c_buf, c_hbm, 0), (f_buf, f_hbm, 1)):
            stores.append(pltpu.make_async_copy(buffer.at[span, :], out.at[span, :], store_sem.at[2 * slot + at]))
        stores[-2].start()
        f_buf[span, :] = advance(c_buf[span, :], win[0], wout[0])
        stores[-1].start()

    finish(mine, 0)

    @pl.when(neither(first))
    def _():
        for share in shares:
            share.wait_recv()

    finish(half - mine, 1)
    share_half.wait_send()

    @pl.when(neither(first))
    def _():
        for share in shares:
            share.wait_send()

    @pl.when(send_map)
    def _():
        share_map.wait_send()
        to_before.wait_send()

    @pl.when(send_x)
    def _():
        x_hop.wait_send()

    @pl.when(recv_x)
    def _():
        for gather in gathers:
            gather.wait_send()
        swap.wait_send()

    @pl.when(send_local)
    def _():
        for hop in local_hops:
            hop.wait_send()

    @pl.when(send_e)
    def _():
        for away in range(1, widest + 1):
            @pl.when(following_size >= away)
            def _(away=away):
                for hop in e_hops[away - 1]:
                    hop.wait_send()

    for store in stores:
        store.wait()


def shards(layers, columns, states, w_in, w_out):
    rows, width = states.shape[1:]
    hidden = w_in.shape[2]
    half = rows // 2
    part = width // (2 * columns)
    widest = max(groups_of(layers // 2)[1:])
    block = jax.ShapeDtypeStruct((rows, width), BF16)
    hbm = pl.BlockSpec(memory_space=pl.ANY)
    dma, vmem = pltpu.SemaphoreType.DMA, pltpu.VMEM
    corrected, fine = pl.pallas_call(
        functools.partial(kernel, layers, columns),
        out_shape=(block, block),
        in_specs=[hbm, hbm, hbm],
        out_specs=(hbm, hbm),
        scratch_shapes=[
            vmem((rows, width), BF16),
            vmem((2, width, hidden), BF16),
            vmem((2, hidden, width), BF16),
            vmem((rows, width), BF16),
            vmem((2, width, width), BF16),
            vmem((width, width), BF16),
            vmem((rows, width), F32),
            vmem((rows, width), BF16),
            vmem((rows, width), BF16),
            vmem((rows, width), F32),
            vmem((half, width), F32),
            vmem((rows, width), BF16),
            vmem((half, width), BF16),
            vmem((half, width), BF16),
            vmem((part, width), BF16),
            vmem((part, width), BF16),
            vmem((width, width), BF16),
            vmem((width, width), BF16),
            vmem((half, width), F32),
            vmem((half, width), BF16),
            vmem((half, width), BF16),
            vmem((rows, width), BF16),
            vmem((rows, width), BF16),
            dma((5,)),
            dma((2,)),
            dma((2,)),
            dma((2,)),
            dma((2,)),
            dma((columns,)),
            dma,
            dma((2,)),
            dma((CHUNKS,)),
            dma((CHUNKS,)),
            dma((widest * CHUNKS,)),
            dma((CHUNKS,)),
            dma((CHUNKS,)),
            dma((CHUNKS,)),
            dma((4,)),
            pltpu.SemaphoreType.REGULAR,
            pltpu.SemaphoreType.REGULAR,
        ],
        compiler_params=pltpu.CompilerParams(
            collective_id=0, has_side_effects=True, vmem_limit_bytes=67043328
        ),
    )(states[0], w_in, w_out)
    return (corrected[None], fine[None])


def solution(mesh):
    return jax.shard_map(
        functools.partial(shards, mesh.shape["layer"], mesh.shape["dp"]),
        mesh=mesh,
        in_specs=(P("layer", "dp", None), P("layer", None, None), P("layer", None, None)),
        out_specs=(P("layer", "dp", None), P("layer", "dp", None)),
        check_vma=False,
    )
```

time: 41.9 us -> 41.8 us (level)
  the two profiles are of different devices: /device:TPU:417 before, /device:TPU:385 now
where the time goes in v3:
time: 41.8 us; the launch traced here: 41.6 us
  Pallas kernels  37.8 us (90%)
  local copies, waits for them, and re-layouts  3.14 us (8%)
  between operations  0.64 us (2%)
    pallas_call x1, Pallas kernels, shards(): pl.pallas_call(functools.partial(kernel, layers, columns), out_shape=(blo...  37.8 us
    unnamed x2, local copies, waits for them, and re-layouts  3.14 us

profile of v3, /device:TPU:385, one launch (start us, length us, event | category | flops | bytes accessed | tf_op | source)
XLA Modules:
  0.0 41.6 jit_solution(821087426800165890)
XLA Ops:
  0.6 37.8 %shard_map.50 = (bf16[128,512]{1,0:T(8,128)(2,1)}, bf16[128,512]{1,0:T(8,128)(2,1)}) custom-call(bf16[128,512]{1,0:T(8,128)(2,1)} %bitcast.3, bf16[2,512,1024]{2,1,0:T(8,128)(2,1)} %win_hbm.1, bf16[2,1024,512]{2,1,0:T(8,128)(2,1)} %wout_hbm.1), custom_call_target="tpu_custom_call" | custom-call | tf_op jit(solution)/shard_map/pallas_call | solution.py:455
  38.5 1.6 %copy.7 = bf16[1,128,512]{2,1,0:T(8,128)(2,1)} copy(bf16[1,128,512]{2,1,0:T(8,128)(2,1)} %bitcast.5) | data formatting | bytes 262144
  40.0 1.6 %copy.8 = bf16[1,128,512]{2,1,0:T(8,128)(2,1)} copy(bf16[1,128,512]{2,1,0:T(8,128)(2,1)} %bitcast.4) | data formatting | bytes 262144

commit v4 on v3

--- a/solution.py
+++ b/solution.py
@@ -14,7 +14,7 @@
 
 def groups_of(chips):
     if chips == 16:
-        return (4, 3, 5, 4)
+        return (4, 4, 5, 3)
     return (chips // 3, chips // 3, chips - 2 * (chips // 3))
 
 
@@ -32,7 +32,7 @@
 
 
 def kernel(
-    layers, columns, states_hbm, win_hbm, wout_hbm, c_hbm, f_hbm,
+    layers, columns, states_hbm, win_hbm, wout_hbm, both_hbm,
     state, win, wout, follow, maps, pair, defect, half_out, half_in, d_all, b_half, carried,
     local_in, local_out, x_in, x_out, prefix, jump, base, e_in, e_out, c_buf, f_buf,
     load_sem, follow_sems, map_sems, half_sems, x_sems, gather_send, gather_recv, swap_sems,
@@ -77,14 +77,14 @@
     loads = [
         pltpu.make_async_copy(source, target, load_sem.at[slot])
         for slot, (source, target) in enumerate((
+            (states_hbm, state),
             (win_hbm.at[0], win.at[0]),
             (wout_hbm.at[0], wout.at[0]),
-            (states_hbm, state),
             (win_hbm.at[1], win.at[1]),
             (wout_hbm.at[1], wout.at[1]),
         ))
     ]
-    for load in loads:
+    for load in loads[:3]:
         load.start()
 
     barrier = pltpu.get_barrier_semaphore()
@@ -120,14 +120,16 @@
             greet(dp=peer)
 
     loads[0].wait()
+    for load in loads[3:]:
+        load.start()
     loads[1].wait()
+    loads[2].wait()
     own_map = maps.at[core]
 
     @pl.when(send_map)
     def _():
         own_map[...] = (0.25 * dot(win[0], wout[0])).astype(BF16)
 
-    loads[2].wait()
     pl.semaphore_wait(
         barrier,
         1 + number(send_back) + number(neither(first)) + number(neither(last))
@@ -151,15 +153,11 @@
             pl.semaphore_signal(plane, inc=1, device_id={"dp": peer})
 
     def pass_hello(turn):
-        @pl.when(both(to_close == turn, neither(first)))
+        @pl.when(both(to_close == turn, later))
         def _():
             if turn > 0:
                 pl.semaphore_wait(hello, 1)
             pl.semaphore_signal(hello, inc=1, device_id={"layer": me - 2})
-
-    @pl.when(both(first, neither(closes)))
-    def _():
-        pl.semaphore_wait(hello, 1)
 
     pass_hello(0)
     relaxed = advance(state[...], win[0], wout[0])
@@ -259,7 +257,8 @@
         for hop in local_hops:
             hop.start()
 
-    pass_hello(4)
+    for turn in range(4, max(sizes)):
+        pass_hello(turn)
 
     @pl.when(recv_x)
     def _():
@@ -304,10 +303,6 @@
                 def _():
                     e_out[span, :] = ahead.astype(BF16)
                     send_far(at)
-
-    @pl.when(both(closes, neither(later)))
-    def _():
-        send_others()
 
     @pl.when(recv_x)
     def _():
@@ -390,13 +385,17 @@
         def _():
             c_buf[span, :] = (state[span, :].astype(F32) + d_all[span, :]).astype(BF16)
 
-        for buffer, out, at in ((c_buf, c_hbm, 0), (f_buf, f_hbm, 1)):
+        for buffer, out, at in ((c_buf, both_hbm.at[0], 0), (f_buf, both_hbm.at[1], 1)):
             stores.append(pltpu.make_async_copy(buffer.at[span, :], out.at[span, :], store_sem.at[2 * slot + at]))
         stores[-2].start()
         f_buf[span, :] = advance(c_buf[span, :], win[0], wout[0])
         stores[-1].start()
 
     finish(mine, 0)
+
+    @pl.when(both(closes, neither(later)))
+    def _():
+        send_others()
 
     @pl.when(neither(first))
     def _():
@@ -452,11 +451,11 @@
     block = jax.ShapeDtypeStruct((rows, width), BF16)
     hbm = pl.BlockSpec(memory_space=pl.ANY)
     dma, vmem = pltpu.SemaphoreType.DMA, pltpu.VMEM
-    corrected, fine = pl.pallas_call(
+    result = pl.pallas_call(
         functools.partial(kernel, layers, columns),
-        out_shape=(block, block),
+        out_shape=jax.ShapeDtypeStruct((2, rows, width), BF16),
         in_specs=[hbm, hbm, hbm],
-        out_specs=(hbm, hbm),
+        out_specs=hbm,
         scratch_shapes=[
             vmem((rows, width), BF16),
             vmem((2, width, hidden), BF16),
@@ -503,7 +502,7 @@
             collective_id=0, has_side_effects=True, vmem_limit_bytes=67043328
         ),
     )(states[0], w_in, w_out)
-    return (corrected[None], fine[None])
+    return (result[0:1], result[1:2])
 
 
 def solution(mesh):

time: 41.8 us -> 38.8 us (0.928)
  the two profiles are of different devices: /device:TPU:385 before, /device:TPU:417 now
where the time goes in v4:
time: 38.8 us; the launch traced here: 38.6 us
  Pallas kernels  36.3 us (94%)
  local copies, waits for them, and re-layouts  1.68 us (4%)
  between operations  0.64 us (2%)
    pallas_call x1, Pallas kernels, shards(): pl.pallas_call(functools.partial(kernel, layers, columns), out_shape=jax....  36.3 us
    slice x1, local copies, waits for them, and re-layouts, shards(): return (result[0:1], result[1:2])  1.68 us

profile of v4, /device:TPU:417, one launch (start us, length us, event | category | flops | bytes accessed | tf_op | source)
XLA Modules:
  0.0 38.6 jit_solution(18301717591774936273)
XLA Ops:
  0.6 36.3 %shard_map.50 = bf16[2,128,512]{2,1,0:T(8,128)(2,1)} custom-call(bf16[128,512]{1,0:T(8,128)(2,1)} %bitcast.1, bf16[2,512,1024]{2,1,0:T(8,128)(2,1)} %win_hbm.1, bf16[2,1024,512]{2,1,0:T(8,128)(2,1)} %wout_hbm.1), custom_call_target="tpu_custom_call" | custom-call | tf_op jit(solution)/shard_map/pallas_call | solution.py:454
  36.9 1.7 %fusion = (bf16[1,128,512]{2,1,0:T(8,128)(2,1)}, bf16[1,128,512]{2,1,0:T(8,128)(2,1)}) fusion(bf16[2,128,512]{2,1,0:T(8,128)(2,1)} %shard_map.50), kind=kLoop, calls=%fused_computation | loop fusion | bytes 524288 | tf_op jit(solution)/shard_map/slice | solution.py:505

commit v5 on v4

--- a/solution.py
+++ b/solution.py
@@ -33,10 +33,10 @@
 
 def kernel(
     layers, columns, states_hbm, win_hbm, wout_hbm, both_hbm,
-    state, win, wout, follow, maps, pair, defect, half_out, half_in, d_all, b_half, carried,
+    state, win, wout, follow, maps, pair, pushed, defect, half_out, half_in, d_all, b_half, carried,
     local_in, local_out, x_in, x_out, prefix, jump, base, e_in, e_out, c_buf, f_buf,
-    load_sem, follow_sems, map_sems, half_sems, x_sems, gather_send, gather_recv, swap_sems,
-    local_send, local_recv, e_send, e_recv, share_send, share_recv, store_sem, hello, plane,
+    load_sem, follow_send, follow_recv, map_send, map_recv, half_send, half_recv, x_sems, gather_send, gather_recv, swap_sems,
+    local_send, local_recv, e_send, e_recv, share_send, share_recv, store_sem, hello, plane, in_plane,
 ):
     me, column = lax.axis_index("layer"), lax.axis_index("dp")
     core, chip = lax.rem(me, 2), me // 2
@@ -65,6 +65,7 @@
     recv_x, send_x = both(recv_local, later), both(send_local, later)
     send_e = both(closes, following_size > 0)
     send_map, recv_map = me > 0, me != 1
+    gate = both(closes, later)
 
     def number(flag):
         return flag.astype(jnp.int32)
@@ -100,13 +101,17 @@
     def _():
         greet(layer=me + 1)
 
-    @pl.when(neither(first))
+    @pl.when(recv_local)
     def _():
         greet(layer=me - 2)
 
-    @pl.when(neither(last))
-    def _():
-        greet(layer=me + 2)
+    @pl.when(both(later, neither(closes)))
+    def _():
+        greet(layer=me + 2 * to_close)
+
+    @pl.when(send_e)
+    def _():
+        greet(layer=me + 2 * following_size)
 
     side = 4 if columns % 4 == 0 else 1
     depth = columns // side
@@ -114,7 +119,7 @@
     in_line = [line * depth + lax.rem(place + turn, depth) for turn in range(1, depth)]
     across = [lax.rem(line + turn, side) * depth + place for turn in range(1, side)]
 
-    @pl.when(recv_x)
+    @pl.when(gate)
     def _():
         for peer in in_line + across:
             greet(dp=peer)
@@ -122,73 +127,109 @@
     loads[0].wait()
     for load in loads[3:]:
         load.start()
-    loads[1].wait()
-    loads[2].wait()
-    own_map = maps.at[core]
-
-    @pl.when(send_map)
-    def _():
-        own_map[...] = (0.25 * dot(win[0], wout[0])).astype(BF16)
+    low, high = pl.ds(0, half_width), pl.ds(half_width, half_width)
+
+    def make_map(span):
+        maps[core, span, :] = (0.25 * dot(win[0, span, :], wout[0])).astype(BF16)
+
+    @pl.when(gate)
+    def _():
+        loads[1].wait()
+        loads[2].wait()
+        make_map(low)
+        make_map(high)
 
     pl.semaphore_wait(
         barrier,
-        1 + number(send_back) + number(neither(first)) + number(neither(last))
-        + number(recv_x) * (len(in_line) + len(across)),
+        1 + number(send_back) + number(send_local) + number(gate) * (size + len(in_line) + len(across)),
     )
-    share_map = remote(own_map, own_map, map_sems.at[0], map_sems.at[1], layer=partner)
-
-    @pl.when(send_map)
-    def _():
-        share_map.start()
-
-    to_before = remote(state, follow, follow_sems.at[0], follow_sems.at[1], layer=me - 1)
+
+    def half_at(offset):
+        return pl.ds(pl.multiple_of(offset, half), half)
+
+    own_rows, other_rows = half_at(mine), half_at(half - mine)
+    to_before = [
+        remote(state.at[span, :], follow.at[span, :], follow_send.at[at], follow_recv.at[at], layer=me - 1)
+        for at, span in enumerate((own_rows, other_rows))
+    ]
+
+    map_hops = [
+        remote(maps.at[core, span, :], maps.at[core, span, :], map_send.at[at], map_recv.at[at], layer=partner)
+        for at, span in enumerate((low, high))
+    ]
+
+    @pl.when(gate)
+    def _():
+        for hop in map_hops:
+            hop.start()
 
     @pl.when(me > 0)
     def _():
-        to_before.start()
-
-    @pl.when(recv_x)
-    def _():
+        for copy in to_before:
+            copy.start()
+
+    @pl.when(neither(gate))
+    def _():
+        loads[1].wait()
+        loads[2].wait()
+
+        @pl.when(send_map)
+        def _():
+            for span, hop in zip((low, high), map_hops):
+                make_map(span)
+                hop.start()
+
+    @pl.when(gate)
+    def _():
+        pl.semaphore_signal(hello, inc=1, device_id={"layer": 2 * (start - 1) + core})
+        for peer in in_line:
+            pl.semaphore_signal(in_plane, inc=1, device_id={"dp": peer})
+
+    relaxed = advance(state[...], win[0], wout[0])
+
+    loads[3].wait()
+    loads[4].wait()
+    pushed[...] = advance(relaxed, win[1], wout[1])
+    share_other, share_own = [
+        remote(half_out.at[span, :], half_in.at[span, :], half_send.at[at], half_recv.at[at], layer=partner)
+        for at, span in enumerate((other_rows, own_rows))
+    ]
+
+    @pl.when(me == layers - 1)
+    def _():
+        follow[...] = jnp.zeros_like(follow)
+
+    def take_defect(at, span):
+        @pl.when(me < layers - 1)
+        def _():
+            to_before[at].wait_recv()
+
+        defect[span, :] = pushed[span, :].astype(F32) - follow[span, :].astype(F32)
+        half_out[span, :] = defect[span, :].astype(BF16)
+
+    take_defect(0, other_rows)
+    share_other.start()
+    take_defect(1, own_rows)
+
+    @pl.when(core == 0)
+    def _():
+        share_own.start()
+
+    @pl.when(gate)
+    def _():
+        if in_line:
+            pl.semaphore_wait(in_plane, len(in_line))
         for peer in across:
             pl.semaphore_signal(plane, inc=1, device_id={"dp": peer})
 
-    def pass_hello(turn):
-        @pl.when(both(to_close == turn, later))
-        def _():
-            if turn > 0:
-                pl.semaphore_wait(hello, 1)
-            pl.semaphore_signal(hello, inc=1, device_id={"layer": me - 2})
-
-    pass_hello(0)
-    relaxed = advance(state[...], win[0], wout[0])
-    pass_hello(1)
-
-    loads[3].wait()
-    loads[4].wait()
-    pushed = advance(relaxed, win[1], wout[1])
-
-    @pl.when(me < layers - 1)
-    def _():
-        to_before.wait_recv()
-
-    @pl.when(me == layers - 1)
-    def _():
-        follow[...] = jnp.zeros_like(follow)
-
-    defect[...] = pushed.astype(F32) - follow[...].astype(F32)
-    half_out[...] = defect[...].astype(BF16)
-    share_half = remote(half_out, half_in, half_sems.at[0], half_sems.at[1], layer=partner)
-    share_half.start()
-    pass_hello(2)
-
     @pl.when(recv_map)
     def _():
-        share_map.wait_recv()
-
-    @pl.when(neither(first))
-    def _():
-        even_map, odd_map = maps[0], maps[1]
-        pair[...] = (even_map.astype(F32) + odd_map.astype(F32) + dot(even_map, odd_map)).astype(BF16)
+        for hop in map_hops:
+            hop.wait_recv()
+
+    def pair_rows(span):
+        ahead = maps[0, span, :].astype(F32) + maps[1, span, :].astype(F32)
+        return (ahead + dot(maps[0, span, :], maps[1])).astype(BF16)
 
     own_part = pl.ds(pl.multiple_of(core * half_width + column * part, part), part)
     x_hop = remote(x_out, x_in, x_sems.at[0], x_sems.at[1], layer=me + 2)
@@ -202,21 +243,50 @@
 
     @pl.when(both(send_x, opens))
     def _():
-        x_out[...] = pair[own_part, :]
+        x_out[...] = pair_rows(own_part)
         x_hop.start()
 
-    pass_hello(3)
-    share_half.wait_recv()
-    own_rows = pl.ds(pl.multiple_of(mine, half), half)
+    @pl.when(neither(first))
+    def _():
+        pair[...] = pair_rows(pl.ds(0, width))
+
+    @pl.when(gate)
+    def _():
+        if across:
+            pl.semaphore_wait(plane, len(across))
+        for turn in range(1, widest - 1):
+            @pl.when(turn < size - 1)
+            def _(turn=turn):
+                pl.semaphore_signal(plane, inc=1, device_id={"layer": me - 2 * turn})
+
+    @pl.when(recv_x)
+    def _():
+        x_hop.wait_recv()
+
+        @pl.when(send_x)
+        def _():
+            x = x_in[...]
+            x_out[...] = (pair[own_part, :].astype(F32) + x.astype(F32) + dot(x, pair[...])).astype(BF16)
+            x_hop.start()
+
+        @pl.when(send_x)
+        def _():
+            pl.semaphore_wait(plane, 1)
+
+        for gather in gathers:
+            gather.start()
+        prefix[own_part, :] = x_in[...]
+
+    share_other.wait_recv()
 
     @pl.when(core == 0)
     def _():
-        d_all[...] = defect[...]
+        d_all[own_rows, :] = defect[own_rows, :]
         b_half[...] = half_in[own_rows, :].astype(F32)
 
     @pl.when(core == 1)
     def _():
-        d_all[...] = half_in[...].astype(F32)
+        d_all[own_rows, :] = half_in[own_rows, :].astype(F32)
         b_half[...] = defect[own_rows, :]
 
     even_half = d_all[own_rows, :]
@@ -251,30 +321,11 @@
                 for hop in e_hops[away - 1]:
                     hop.start()
 
-    @pl.when(opens)
+    @pl.when(both(opens, send_local))
     def _():
         local_out[...] = b_half[...].astype(BF16)
         for hop in local_hops:
             hop.start()
-
-    for turn in range(4, max(sizes)):
-        pass_hello(turn)
-
-    @pl.when(recv_x)
-    def _():
-        x_hop.wait_recv()
-
-        @pl.when(send_x)
-        def _():
-            x = x_in[...]
-            x_out[...] = (pair[own_part, :].astype(F32) + x.astype(F32) + dot(x, pair[...])).astype(BF16)
-            x_hop.start()
-
-        if across:
-            pl.semaphore_wait(plane, len(across))
-        for gather in gathers:
-            gather.start()
-        prefix[own_part, :] = x_in[...]
 
     @pl.when(send_e)
     def _():
@@ -402,8 +453,17 @@
         for share in shares:
             share.wait_recv()
 
+    @pl.when(core == 1)
+    def _():
+        share_own.wait_recv()
+        d_all[other_rows, :] = half_in[other_rows, :].astype(F32)
+
     finish(half - mine, 1)
-    share_half.wait_send()
+    share_other.wait_send()
+
+    @pl.when(core == 0)
+    def _():
+        share_own.wait_send()
 
     @pl.when(neither(first))
     def _():
@@ -412,8 +472,10 @@
 
     @pl.when(send_map)
     def _():
-        share_map.wait_send()
-        to_before.wait_send()
+        for hop in map_hops:
+            hop.wait_send()
+        for copy in to_before:
+            copy.wait_send()
 
     @pl.when(send_x)
     def _():
@@ -463,6 +525,7 @@
             vmem((rows, width), BF16),
             vmem((2, width, width), BF16),
             vmem((width, width), BF16),
+            vmem((rows, width), BF16),
             vmem((rows, width), F32),
             vmem((rows, width), BF16),
             vmem((rows, width), BF16),
@@ -485,6 +548,9 @@
             dma((2,)),
             dma((2,)),
             dma((2,)),
+            dma((2,)),
+            dma((2,)),
+            dma((2,)),
             dma((columns,)),
             dma,
             dma((2,)),
@@ -497,6 +563,7 @@
             dma((4,)),
             pltpu.SemaphoreType.REGULAR,
             pltpu.SemaphoreType.REGULAR,
+            pltpu.SemaphoreType.REGULAR,
         ],
         compiler_params=pltpu.CompilerParams(
             collective_id=0, has_side_effects=True, vmem_limit_bytes=67043328

time: 38.8 us -> 38.4 us (0.990)
  the two profiles are of different devices: /device:TPU:417 before, /device:TPU:425 now
where the time goes in v5:
time: 38.4 us; the launch traced here: 38.3 us
  Pallas kernels  36 us (94%)
  local copies, waits for them, and re-layouts  1.68 us (4%)
  between operations  0.64 us (2%)
    pallas_call x1, Pallas kernels, shards(): pl.pallas_call(functools.partial(kernel, layers, columns), out_shape=jax....  36 us
    slice x1, local copies, waits for them, and re-layouts, shards(): return (result[0:1], result[1:2])  1.68 us

profile of v5, /device:TPU:425, one launch (start us, length us, event | category | flops | bytes accessed | tf_op | source)
XLA Modules:
  0.0 38.3 jit_solution(869782362710337801)
XLA Ops:
  0.6 36.0 %shard_map.50 = bf16[2,128,512]{2,1,0:T(8,128)(2,1)} custom-call(bf16[128,512]{1,0:T(8,128)(2,1)} %bitcast.1, bf16[2,512,1024]{2,1,0:T(8,128)(2,1)} %win_hbm.1, bf16[2,1024,512]{2,1,0:T(8,128)(2,1)} %wout_hbm.1), custom_call_target="tpu_custom_call" | custom-call | tf_op jit(solution)/shard_map/pallas_call | solution.py:516
  36.6 1.7 %fusion = (bf16[1,128,512]{2,1,0:T(8,128)(2,1)}, bf16[1,128,512]{2,1,0:T(8,128)(2,1)}) fusion(bf16[2,128,512]{2,1,0:T(8,128)(2,1)} %shard_map.50), kind=kLoop, calls=%fused_computation | loop fusion | bytes 524288 | tf_op jit(solution)/shard_map/slice | solution.py:572

commit v6 on v5

--- a/solution.py
+++ b/solution.py
@@ -309,6 +309,8 @@
     ]
 
     def send_far(at):
+        if at == 0:
+            pl.semaphore_wait(hello, 1)
         for away in range(1, widest + 1):
             @pl.when(following_size == away)
             def _(away=away):
@@ -326,10 +328,6 @@
         local_out[...] = b_half[...].astype(BF16)
         for hop in local_hops:
             hop.start()
-
-    @pl.when(send_e)
-    def _():
-        pl.semaphore_wait(hello, 1)
 
     @pl.when(recv_local)
     def _():

time: 38.4 us -> 38.5 us (level)
  no operation moved by 1% of the time
where the time goes in v6:
time: 38.5 us; the launch traced here: 38.3 us
  Pallas kernels  36 us (94%)
  local copies, waits for them, and re-layouts  1.68 us (4%)
  between operations  0.64 us (2%)
    pallas_call x1, Pallas kernels, shards(): pl.pallas_call(functools.partial(kernel, layers, columns), out_shape=jax....  36 us
    slice x1, local copies, waits for them, and re-layouts, shards(): return (result[0:1], result[1:2])  1.68 us

profile of v6, /device:TPU:425, one launch (start us, length us, event | category | flops | bytes accessed | tf_op | source)
XLA Modules:
  0.0 38.3 jit_solution(8960992007061524667)
XLA Ops:
  0.6 36.0 %shard_map.50 = bf16[2,128,512]{2,1,0:T(8,128)(2,1)} custom-call(bf16[128,512]{1,0:T(8,128)(2,1)} %bitcast.1, bf16[2,512,1024]{2,1,0:T(8,128)(2,1)} %win_hbm.1, bf16[2,1024,512]{2,1,0:T(8,128)(2,1)} %wout_hbm.1), custom_call_target="tpu_custom_call" | custom-call | tf_op jit(solution)/shard_map/pallas_call | solution.py:514
  36.6 1.7 %fusion = (bf16[1,128,512]{2,1,0:T(8,128)(2,1)}, bf16[1,128,512]{2,1,0:T(8,128)(2,1)}) fusion(bf16[2,128,512]{2,1,0:T(8,128)(2,1)} %shard_map.50), kind=kLoop, calls=%fused_computation | loop fusion | bytes 524288 | tf_op jit(solution)/shard_map/slice | solution.py:570
